TPU v7x, 256 devices: a whole 4x4x8 slice. The times are simulated.
256 devices in a mesh: wide: 64 (over y, x, z_lo), narrow: 4 (over z_hi, core).
Axes of the slice: x: 4, y: 4, z: 8 (z_hi: 2, z_lo: 4; z = z_hi * 4 + z_lo), core: 2. Of those that a mesh axis runs over, the one named last changes fastest.
Arguments:
- volume: float32 [1024, 48, 1024], P('wide', None, 'narrow'), may hold values from 0 to 2
- codes_in: bfloat16 [1024, 72, 1536], P('wide', None, 'narrow'), may hold values from -4 to 4
- x_transform: float32 [1024, 1024], replicated, may hold values from -1 to 1, as said below
- y_atoms: bfloat16 [1024, 1536], replicated, may hold values from -0.1875 to 0.1875
- de_atoms: bfloat16 [48, 72], replicated, may hold values from -0.875 to 0.875
Outputs:
- codes_out: bfloat16 [1024, 72, 1536], P('wide', None, 'narrow')
- estimate: bfloat16 [1024, 48, 1024], P('wide', None, 'narrow')
Inputs may be any that keep to these rules, and one draw needn't show every extreme that they name: x_transform is orthonormal: its transpose is its inverse.
All inputs are finite; a program needn't handle non-finite values.
Results may differ from a plain program's by a relative error of at most 0.0065.
Values may be sent and summed in bfloat16 or wider, within the bound.
A program may use at most 64 MiB of HBM per device.

v0:
```python
import jax
import jax.numpy as jnp
from jax import lax
from jax.sharding import PartitionSpec as P

step_size = 0.06
threshold = 0.05
best = lax.Precision.HIGHEST


def shards(volume, codes_in, x_transform, y_atoms, de_atoms):
    xrows, depth, ylocal = volume.shape
    klocal = codes_in.shape[2]
    where = lax.axis_index("narrow")
    y_rows = lax.dynamic_slice_in_dim(y_atoms, where * ylocal, ylocal, 0)
    y_cols = lax.dynamic_slice_in_dim(y_atoms, where * klocal, klocal, 1)
    de_wide = de_atoms.astype(jnp.float32)

    def apply_x(columns, forward):
        if forward:
            return jnp.dot(x_transform, columns, precision=best)
        return lax.dot_general(x_transform, columns, (((0,), (0,)), ((), ())), precision=best)

    def along_x(field, forward):
        flat = field.reshape(xrows, depth * ylocal)
        columns = lax.all_to_all(flat, "wide", split_axis=1, concat_axis=0, tiled=True)
        mixed = apply_x(columns, forward)
        returned = lax.all_to_all(mixed, "wide", split_axis=0, concat_axis=1, tiled=True)
        return returned.reshape(xrows, depth, ylocal)

    def rebuild(codes):
        atoms = jnp.einsum(
            "fk,bkc->bfc", de_atoms, codes, preferred_element_type=jnp.float32
        ).astype(jnp.bfloat16)
        return jnp.einsum(
            "bfc,yc->bfy",
            lax.all_gather(atoms, "narrow", axis=2, tiled=True),
            y_rows,
            preferred_element_type=jnp.float32,
        )

    target = along_x(volume, True)
    codes = codes_in
    misfit = rebuild(codes) - target
    pulled = jnp.einsum("fk,bfy->bky", de_wide, misfit, precision=best).astype(jnp.bfloat16)
    grads = jnp.einsum(
        "bky,yc->bkc",
        lax.all_gather(pulled, "narrow", axis=2, tiled=True),
        y_cols,
        preferred_element_type=jnp.float32,
    )
    moved = codes.astype(jnp.float32) - step_size * grads
    codes = (moved - jnp.clip(moved, -threshold, threshold)).astype(jnp.bfloat16)
    image = rebuild(codes)
    estimate = jnp.maximum(along_x(image, False), 0.0).astype(jnp.bfloat16)
    return (codes, estimate)


def solution(mesh):
    return jax.shard_map(
        shards,
        mesh=mesh,
        in_specs=(P("wide", None, "narrow"), P("wide", None, "narrow"), P(), P(), P()),
        out_specs=(P("wide", None, "narrow"), P("wide", None, "narrow")),
        check_vma=False,
    )
```

profile of v0, /device:TPU:1, one launch (start us, length us, event | category | flops | bytes accessed | tf_op | source)
XLA Modules:
  0.0 301.2 jit_solution(1969324107720229944)
XLA Ops:
  7.2 0.0 all-gather.4.cloned.1.call-start
  7.2 2.5 fusion.2
  9.7 0.0 all-gather.4.cloned.1.call-update
  9.7 2.5 all_to_all.48
  12.2 2.0 copy.14
  14.2 66.0 %all_to_all.64 = f32[16,64,192]{2,0,1:T(8,128)S(1)} all-to-all(f32[16,64,192]{2,0,1:T(8,128)S(1)} %copy.14), channel_id=1, replica_groups=mesh['wide'=64,'narrow'=4] {'wide'}, dimensions={1} | all-to-all | bytes 1572864 | tf_op jit(solution)/shard_map/all_to_all | solution.py:26
  80.3 4.4 %fusion.18 = f32[64,16,192]{2,1,0:T(8,128)} fusion(f32[64,16,1024]{2,1,0:T(8,128)S(1)} %bitcast.46, f32[1024,192,1]{1,0,2:T(8,128)S(1)} %bitcast.47), kind=kOutput, calls=%fused_computation.25 | convolution fusion | flops 2415919104 | bytes 5767168 | tf_op jit(solution)/shard_map/dot_general | solution.py:21
  84.6 5.6 %all-to-all-start.1 = ((f32[64,16,192]{2,1,0:T(8,128)}), f32[64,16,192]{2,1,0:T(8,128)}, u32[]{:S(2)}, u32[]{:S(2)}) async-start(f32[64,16,192]{2,1,0:T(8,128)} %fusion.18), calls=%async_computation.1 | async-start | bytes 2097152 | tf_op jit(solution)/shard_map/all_to_all | solution.py:28
  90.3 0.0 all-gather.6.cloned.1.call-start
  90.3 28.1 %all-to-all-done.1 = f32[64,16,192]{2,1,0:T(8,128)} async-done(((f32[64,16,192]{2,1,0:T(8,128)}), f32[64,16,192]{2,1,0:T(8,128)}, u32[]{:S(2)}, u32[]{:S(2)}) %all-to-all-start.1) | async-done | bytes 786464 | tf_op jit(solution)/shard_map/all_to_all | solution.py:28
  118.5 2.8 copy.16
  121.3 2.7 reshape.30
  124.0 2.7 convolution_subtract_fusion
  126.7 1.5 fusion.1
  128.2 0.0 all-gather.6.cloned.1.call-update
  128.2 0.2 all-gather.8.cloned.1.call-start
  128.4 45.1 %all-gather.6.cloned.1.call-done = bf16[16,72,1024]{2,1,0:T(8,128)(2,1)} async-done(((bf16[16,72,256]{2,1,0:T(8,128)(2,1)}), bf16[16,72,1024]{2,1,0:T(8,128)(2,1)}) %all-gather.6.cloned.1.call-update) | async-done | bytes 2359312 | tf_op jit(solution)/shard_map/all_gather | solution.py:48
  173.5 3.3 %fusion = bf16[16,72,384]{2,1,0:T(8,128)(2,1)S(1)} fusion(bf16[16,72,384]{2,1,0:T(8,128)(2,1)} %param.6, bf16[16,72,1024]{2,1,0:T(8,128)(2,1)} %all-gather.6.cloned.1.call-done, bf16[1024,1536]{1,0:T(8,128)(2,1)S(1)} %copy-done, s32[]{:T(128)S(6)} %select_n.7), kind=kOutput, calls=%fused_computation.1 | convolution fusion | flops 908623872 | bytes 4915204 | tf_op jit(solution)/shard_map/bky,yc->bkc/dot_general | solution.py:46
  176.9 0.9 copy-done.3
  177.8 1.1 fusion.3
  179.0 0.0 all-gather.8.cloned.1.call-update
  179.0 42.3 %all-gather.8.cloned.1.call-done = bf16[16,48,1536]{2,1,0:T(8,128)(2,1)} async-done(((bf16[16,48,384]{2,1,0:T(8,128)(2,1)}), bf16[16,48,1536]{2,1,0:T(8,128)(2,1)}) %all-gather.8.cloned.1.call-update) | async-done | bytes 2359312 | tf_op jit(solution)/shard_map/all_gather | solution.py:37
  221.3 3.4 %fusion.5 = f32[16,48,256]{2,1,0:T(8,128)} fusion(bf16[16,48,1536]{2,1,0:T(8,128)(2,1)} %all-gather.8.cloned.1.call-done, bf16[1024,1536]{1,0:T(8,128)(2,1)S(1)} %copy-done, s32[]{:T(128)S(6)} %select_n.6), kind=kOutput, calls=%fused_computation.12 | convolution fusion | flops 603979776 | bytes 3932164 | tf_op jit(solution)/shard_map/bfc,yc->bfy/dot_general | solution.py:35
  224.7 2.5 all_to_all.54
  227.2 2.0 copy.17
  229.2 35.8 %all_to_all.65 = f32[16,64,192]{2,0,1:T(8,128)S(1)} all-to-all(f32[16,64,192]{2,0,1:T(8,128)S(1)} %copy.17), channel_id=1, replica_groups=mesh['wide'=64,'narrow'=4] {'wide'}, dimensions={1} | all-to-all | bytes 1572864 | tf_op jit(solution)/shard_map/all_to_all | solution.py:26
  265.0 3.0 convolution_bitcast_fusion
  268.0 1.0 copy.18
  269.0 22.1 %all_to_all.66 = bf16[64,16,192]{2,1,0:T(8,128)(2,1)S(1)} all-to-all(bf16[64,16,192]{2,1,0:T(8,128)(2,1)} %bitcast.49), channel_id=1, replica_groups=mesh['wide'=64,'narrow'=4] {'wide'}, dimensions={0} | all-to-all | bytes 786432 | tf_op jit(solution)/shard_map/all_to_all | solution.py:28
  291.1 0.1 fusion.11
  291.2 0.9 copy.19
  292.1 2.5 convert_element_type.44
  (10 shorter events, 0.0 us)
Async XLA Ops:
  7.2 116.9 %copy-start = (bf16[1024,1536]{1,0:T(8,128)(2,1)S(1)}, bf16[1024,1536]{1,0:T(8,128)(2,1)}, u32[]{:S(2)}) copy-start(bf16[1024,1536]{1,0:T(8,128)(2,1)} %param.8) | copy-start | bytes 9437188
  7.2 116.8 %all-gather.4.cloned.1.call-start = ((), (), s32[]{:S(2)}) async-start(), calls=%async_computation.4 | async-start | bytes 2949120 | tf_op jit(solution)/shard_map/all_gather | solution.py:37
  12.2 68.0 %copy-start.1 = (f32[1024,1024]{1,0:T(8,128)S(1)}, f32[1024,1024]{1,0:T(8,128)}, u32[]{:S(2)}) copy-start(f32[1024,1024]{1,0:T(8,128)} %param.7) | copy-start | bytes 12582916
  84.6 33.8 %all-to-all-start.1 = ((f32[64,16,192]{2,1,0:T(8,128)}), f32[64,16,192]{2,1,0:T(8,128)}, u32[]{:S(2)}, u32[]{:S(2)}) async-start(f32[64,16,192]{2,1,0:T(8,128)} %fusion.18), calls=%async_computation.1 | async-start | bytes 2097152 | tf_op jit(solution)/shard_map/all_to_all | solution.py:28
  90.3 83.3 %all-gather.6.cloned.1.call-start = ((), (), s32[]{:S(2)}) async-start(), calls=%async_computation.5 | async-start | bytes 2949120 | tf_op jit(solution)/shard_map/all_gather | solution.py:48
  124.0 2.7 copy-start.4
  128.2 93.1 %all-gather.8.cloned.1.call-start = ((), (), s32[]{:S(2)}) async-start(), calls=%async_computation.6 | async-start | bytes 2949120 | tf_op jit(solution)/shard_map/all_gather | solution.py:37
  176.9 0.9 copy-start.3
  227.2 37.8 %copy-start.2 = (f32[1024,1024]{1,0:T(8,128)S(1)}, f32[1024,1024]{1,0:T(8,128)}, u32[]{:S(2)}) copy-start(f32[1024,1024]{1,0:T(8,128)} %param.7) | copy-start | bytes 12582916
Sparse Core Ops, SparseCore 0:
  9.8 60.9 all-gather.3
  128.3 45.1 all-gather.5
  179.1 42.1 all-gather.7
where the time goes:
time: 302 us; the launch traced here: 301 us
  blocking collectives  124 us (41%)
  waiting for transfers between devices  116 us (38%)
  matrix products  21.8 us (7%)
  local copies, waits for them, and re-layouts  19.9 us (7%)
  between operations  13.8 us (5%)
  starting transfers between devices  5.94 us (2%)
    all_to_all x2, blocking collectives, along_x(): lax.all_to_all(flat, 'wide', split_axis=1, concat_axis=0, tiled=True)  102 us
    all_gather x1, waiting for transfers between devices, shards(): lax.all_gather(pulled, 'narrow', axis=2, tiled=True)  45.1 us
    all_gather x2, waiting for transfers between devices, rebuild(): lax.all_gather(atoms, 'narrow', axis=2, tiled=True)  42.3 us
    all_to_all x1, waiting for transfers between devices, along_x(): lax.all_to_all(mixed, 'wide', split_axis=0, concat_axis=1, tiled=True)  28.1 us
    all_to_all x1, blocking collectives, along_x(): lax.all_to_all(mixed, 'wide', split_axis=0, concat_axis=1, tiled=True)  22.1 us
    all_to_all x4, local copies, waits for them, and re-layouts, along_x(): lax.all_to_all(flat, 'wide', split_axis=1, concat_axis=0, tiled=True)  8.96 us
  transfers between devices with their start and end apart: 4, of which 3 were waited for; matrix products, arithmetic and copies ran while one was open for 4% of the time, Pallas kernels for 0%

commit v1 on v0

--- a/solution.py
+++ b/solution.py
@@ -6,6 +6,13 @@
 step_size = 0.06
 threshold = 0.05
 best = lax.Precision.HIGHEST
+
+
+def swapped_in(value, axis, dim):
+    devices = lax.axis_size(axis)
+    parts = jnp.stack([value for _ in range(devices)])
+    parts = lax.all_to_all(parts, axis, split_axis=0, concat_axis=0)
+    return jnp.concatenate(parts, axis=dim)
 
 
 def shards(volume, codes_in, x_transform, y_atoms, de_atoms):
@@ -44,10 +51,7 @@
     misfit = rebuild(codes) - target
     pulled = jnp.einsum("fk,bfy->bky", de_wide, misfit, precision=best).astype(jnp.bfloat16)
     grads = jnp.einsum(
-        "bky,yc->bkc",
-        lax.all_gather(pulled, "narrow", axis=2, tiled=True),
-        y_cols,
-        preferred_element_type=jnp.float32,
+        "bky,yc->bkc", swapped_in(pulled, "narrow", 2), y_cols, preferred_element_type=jnp.float32
     )
     moved = codes.astype(jnp.float32) - step_size * grads
     codes = (moved - jnp.clip(moved, -threshold, threshold)).astype(jnp.bfloat16)

time: 302 us -> 321 us (1.063)
  waiting for transfers between devices: 116 us -> 125 us
  starting transfers between devices: 5.94 us -> 14.5 us
  local copies, waits for them, and re-layouts: 19.9 us -> 23.5 us
    all_to_all x0 -> x1, waiting for transfers between devices: none -> 54.9 us  [swapped_in(): parts = lax.all_to_all(parts, axis, split_axis=0, concat_axis=0)]
    all_gather x1 -> x0, waiting for transfers between devices: 45.1 us -> none  [shards(): lax.all_gather(pulled, 'narrow', axis=2, tiled=True)]
    all_to_all x0 -> x1, starting transfers between devices: none -> 8.84 us  [swapped_in(): parts = lax.all_to_all(parts, axis, split_axis=0, concat_axis=0)]
where the time goes in v1:
time: 321 us; the launch traced here: 320 us
  waiting for transfers between devices  125 us (39%)
  blocking collectives  124 us (39%)
  local copies, waits for them, and re-layouts  23.5 us (7%)
  matrix products  19.2 us (6%)
  starting transfers between devices  14.5 us (5%)
  between operations  14.1 us (4%)
    all_to_all x2, blocking collectives, along_x(): lax.all_to_all(flat, 'wide', split_axis=1, concat_axis=0, tiled=True)  102 us
    all_to_all x1, waiting for transfers between devices, swapped_in(): parts = lax.all_to_all(parts, axis, split_axis=0, concat_axis=0)  54.9 us
    all_gather x2, waiting for transfers between devices, rebuild(): lax.all_gather(atoms, 'narrow', axis=2, tiled=True)  41.8 us
    all_to_all x1, waiting for transfers between devices, along_x(): lax.all_to_all(mixed, 'wide', split_axis=0, concat_axis=1, tiled=True)  28.2 us
    all_to_all x1, blocking collectives, along_x(): lax.all_to_all(mixed, 'wide', split_axis=0, concat_axis=1, tiled=True)  22.1 us
    all_to_all x4, local copies, waits for them, and re-layouts, along_x(): lax.all_to_all(flat, 'wide', split_axis=1, concat_axis=0, tiled=True)  8.96 us
    all_to_all x1, starting transfers between devices, swapped_in(): parts = lax.all_to_all(parts, axis, split_axis=0, concat_axis=0)  8.84 us
  transfers between devices with their start and end apart: 4, of which 3 were waited for; matrix products, arithmetic and copies ran while one was open for 4% of the time, Pallas kernels for 0%

profile of v1, /device:TPU:1, one launch (start us, length us, event | category | flops | bytes accessed | tf_op | source)
XLA Modules:
  0.0 320.2 jit_solution(7997671289831284637)
XLA Ops:
  7.2 0.0 all-gather.3.cloned.1.call-start
  7.2 2.5 fusion.2
  9.7 0.0 all-gather.3.cloned.1.call-update
  9.7 2.5 all_to_all.51
  12.2 2.0 copy.20
  14.2 66.0 %all_to_all.69 = f32[16,64,192]{2,0,1:T(8,128)S(1)} all-to-all(f32[16,64,192]{2,0,1:T(8,128)S(1)} %copy.20), channel_id=1, replica_groups=mesh['wide'=64,'narrow'=4] {'wide'}, dimensions={1} | all-to-all | bytes 1572864 | tf_op jit(solution)/shard_map/all_to_all | solution.py:33
  80.3 4.4 %fusion.18 = f32[64,16,192]{2,1,0:T(8,128)} fusion(f32[64,16,1024]{2,1,0:T(8,128)S(1)} %bitcast.49, f32[1024,192,1]{1,0,2:T(8,128)S(1)} %bitcast.50), kind=kOutput, calls=%fused_computation.25 | convolution fusion | flops 2415919104 | bytes 5767168 | tf_op jit(solution)/shard_map/dot_general | solution.py:28
  84.6 5.6 %all-to-all-start.1 = ((f32[64,16,192]{2,1,0:T(8,128)}), f32[64,16,192]{2,1,0:T(8,128)}, u32[]{:S(2)}, u32[]{:S(2)}) async-start(f32[64,16,192]{2,1,0:T(8,128)} %fusion.18), calls=%async_computation.1 | async-start | bytes 2097152 | tf_op jit(solution)/shard_map/all_to_all | solution.py:35
  90.3 28.2 %all-to-all-done.1 = f32[64,16,192]{2,1,0:T(8,128)} async-done(((f32[64,16,192]{2,1,0:T(8,128)}), f32[64,16,192]{2,1,0:T(8,128)}, u32[]{:S(2)}, u32[]{:S(2)}) %all-to-all-start.1) | async-done | bytes 786464 | tf_op jit(solution)/shard_map/all_to_all | solution.py:35
  118.5 2.8 copy.22
  121.3 2.7 reshape.38
  124.0 2.7 convolution_subtract_fusion
  126.7 0.7 fusion.1
  127.4 1.6 stack.2
  128.9 8.8 %all-to-all-start.2 = ((bf16[4,16,72,256]{3,2,1,0:T(8,128)(2,1)}), bf16[4,16,72,256]{3,2,1,0:T(8,128)(2,1)}, u32[]{:S(2)}, u32[]{:S(2)}) async-start(bf16[4,16,72,256]{3,2,1,0:T(8,128)(2,1)} %stack.2), calls=%async_computation.2 | async-start | bytes 4718592 | tf_op jit(solution)/shard_map/all_to_all | solution.py:14
  137.8 54.9 %all-to-all-done.2 = bf16[4,16,72,256]{3,2,1,0:T(8,128)(2,1)} async-done(((bf16[4,16,72,256]{3,2,1,0:T(8,128)(2,1)}), bf16[4,16,72,256]{3,2,1,0:T(8,128)(2,1)}, u32[]{:S(2)}, u32[]{:S(2)}) %all-to-all-start.2) | async-done | bytes 2359328 | tf_op jit(solution)/shard_map/all_to_all | solution.py:14
  192.6 2.1 copy.29
  194.7 1.5 fusion
  196.2 0.9 copy-done.4
  197.1 1.1 fusion.3
  198.3 0.0 all-gather.5.cloned.1.call-update
  198.3 41.8 %all-gather.5.cloned.1.call-done = bf16[16,48,1536]{2,1,0:T(8,128)(2,1)} async-done(((bf16[16,48,384]{2,1,0:T(8,128)(2,1)}), bf16[16,48,1536]{2,1,0:T(8,128)(2,1)}) %all-gather.5.cloned.1.call-update) | async-done | bytes 2359312 | tf_op jit(solution)/shard_map/all_gather | solution.py:44
  240.1 3.4 %fusion.5 = f32[16,48,256]{2,1,0:T(8,128)} fusion(bf16[16,48,1536]{2,1,0:T(8,128)(2,1)} %all-gather.5.cloned.1.call-done, bf16[1024,1536]{1,0:T(8,128)(2,1)S(1)} %copy-done, s32[]{:T(128)S(6)} %select_n.6), kind=kOutput, calls=%fused_computation.12 | convolution fusion | flops 603979776 | bytes 3932164 | tf_op jit(solution)/shard_map/bfc,yc->bfy/dot_general | solution.py:42
  243.5 2.5 all_to_all.58
  245.9 2.0 copy.24
  247.9 35.8 %all_to_all.70 = f32[16,64,192]{2,0,1:T(8,128)S(1)} all-to-all(f32[16,64,192]{2,0,1:T(8,128)S(1)} %copy.24), channel_id=1, replica_groups=mesh['wide'=64,'narrow'=4] {'wide'}, dimensions={1} | all-to-all | bytes 1572864 | tf_op jit(solution)/shard_map/all_to_all | solution.py:33
  283.7 3.0 convolution_bitcast_fusion
  286.7 1.0 copy.25
  287.7 22.1 %all_to_all.71 = bf16[64,16,192]{2,1,0:T(8,128)(2,1)S(1)} all-to-all(bf16[64,16,192]{2,1,0:T(8,128)(2,1)} %bitcast.53), channel_id=1, replica_groups=mesh['wide'=64,'narrow'=4] {'wide'}, dimensions={0} | all-to-all | bytes 786432 | tf_op jit(solution)/shard_map/all_to_all | solution.py:35
  309.8 0.1 fusion.11
  309.9 0.9 copy.26
  310.9 2.5 convert_element_type.44
  (13 shorter events, 0.0 us)
Async XLA Ops:
  7.2 116.9 %copy-start = (bf16[1024,1536]{1,0:T(8,128)(2,1)S(1)}, bf16[1024,1536]{1,0:T(8,128)(2,1)}, u32[]{:S(2)}) copy-start(bf16[1024,1536]{1,0:T(8,128)(2,1)} %param.8) | copy-start | bytes 9437188
  7.2 116.8 %all-gather.3.cloned.1.call-start = ((), (), s32[]{:S(2)}) async-start(), calls=%async_computation.5 | async-start | bytes 2949120 | tf_op jit(solution)/shard_map/all_gather | solution.py:44
  12.2 68.0 %copy-start.1 = (f32[1024,1024]{1,0:T(8,128)S(1)}, f32[1024,1024]{1,0:T(8,128)}, u32[]{:S(2)}) copy-start(f32[1024,1024]{1,0:T(8,128)} %param.7) | copy-start | bytes 12582916
  84.6 33.8 %all-to-all-start.1 = ((f32[64,16,192]{2,1,0:T(8,128)}), f32[64,16,192]{2,1,0:T(8,128)}, u32[]{:S(2)}, u32[]{:S(2)}) async-start(f32[64,16,192]{2,1,0:T(8,128)} %fusion.18), calls=%async_computation.1 | async-start | bytes 2097152 | tf_op jit(solution)/shard_map/all_to_all | solution.py:35
  124.0 2.7 copy-start.5
  128.9 63.7 %all-to-all-start.2 = ((bf16[4,16,72,256]{3,2,1,0:T(8,128)(2,1)}), bf16[4,16,72,256]{3,2,1,0:T(8,128)(2,1)}, u32[]{:S(2)}, u32[]{:S(2)}) async-start(bf16[4,16,72,256]{3,2,1,0:T(8,128)(2,1)} %stack.2), calls=%async_computation.2 | async-start | bytes 4718592 | tf_op jit(solution)/shard_map/all_to_all | solution.py:14
  137.8 102.3 %all-gather.5.cloned.1.call-start = ((), (), s32[]{:S(2)}) async-start(), calls=%async_computation.6 | async-start | bytes 2949120 | tf_op jit(solution)/shard_map/all_gather | solution.py:44
  192.6 2.1 copy-start.3
  196.2 0.9 copy-start.4
  245.9 37.8 %copy-start.2 = (f32[1024,1024]{1,0:T(8,128)S(1)}, f32[1024,1024]{1,0:T(8,128)}, u32[]{:S(2)}) copy-start(f32[1024,1024]{1,0:T(8,128)} %param.7) | copy-start | bytes 12582916
Sparse Core Ops, SparseCore 0:
  9.8 60.9 all-gather.2
  198.4 41.6 all-gather.4
